TPU v7x, 128 devices: a whole 4x4x4 slice. The times are simulated.
128 devices in a mesh: sens: 8 (over z, core), layer: 16 (over y, x).
Axes of the slice: x: 4, y: 4, z: 4, core: 2. Of those that a mesh axis runs over, the one named last changes fastest.
Arguments:
- slopes: bfloat16 [1024, 63600], P('layer', 'sens'), may hold values from -7 to 7
- valid: int32 [63600], P('sens'), may hold values from 0 to 1
- sensor_map: int32 [63600], P('sens'), may hold values from 0 to 5, as said below
- reconstructor: bfloat16 [16000, 63600], P('layer', 'sens'), may hold values from -0.0234375 to 0.0234375
- fitting: bfloat16 [7800, 16000], P('sens', 'layer'), may hold values from -0.046875 to 0.046875
Outputs:
- commands: float32 [1024, 7800], P(('sens', 'layer'))
Inputs may be any that keep to these rules, and one draw needn't show every extreme that they name: `sensor_map`: both slopes of a subaperture (indices 2 i and 2 i + 1) belong to one sensor.
All inputs are finite; a program needn't handle non-finite values.
Results may differ from a plain program's by a relative error of at most 0.02.
Values may be sent and summed in bfloat16 or wider, within the bound.
No kernel may reach another device: no remote copies, remote signals or barrier semaphores. Data moves between devices by JAX's collectives and lax.ppermute only.
A program may use at most 192 MiB of HBM per device.

v0:
```python
import jax
import jax.numpy as jnp
from jax import lax
from jax.sharding import PartitionSpec as P

SENSORS = 6


def copy_for_each(x, axis):
    length = lax.axis_size(axis)
    return lax.all_to_all(jnp.broadcast_to(x[None], (length, *x.shape)), axis, 0, 0, tiled=True)


def taken_together(x, axis):
    everything = copy_for_each(x, axis)
    return jnp.sum(everything.astype(jnp.float32), axis=0)


def cut_along(x, dim, length):
    dims = x.shape
    blocks = x.reshape(*dims[:dim], length, dims[dim] // length, *dims[dim + 1 :])
    return jnp.moveaxis(blocks, dim, 0)


def summed_on_arrival(x, axis, dim):
    blocks = cut_along(x, dim, lax.axis_size(axis))
    arrived = lax.all_to_all(blocks, axis, split_axis=0, concat_axis=0, tiled=True)
    return arrived.astype(jnp.float32).sum(axis=0)


def contract(left, right):
    return lax.dot_general(
        left, right, (((1,), (1,)), ((), ())), preferred_element_type=jnp.float32
    )


def cleaned(block, live, onehot_full, sums, counts):
    means = sums / jnp.maximum(counts, 1.0)
    spread = lax.dot_general(
        means, onehot_full, (((1,), (1,)), ((), ())), precision=lax.Precision.HIGHEST
    )
    return (live.astype(jnp.float32)[None, :] * (block.astype(jnp.float32) - spread)).astype(
        jnp.bfloat16
    )


def per_device(slopes, valid, sensor_map, reconstructor, fitting):
    width_local = slopes.shape[1]
    start = lax.axis_index("sens") * width_local
    parity = (lax.iota(jnp.int32, width_local) + start) % 2
    group = sensor_map * 2 + parity
    labels = lax.iota(jnp.int32, 2 * SENSORS)
    onehot_full = (group[:, None] == labels[None, :]).astype(jnp.float32)
    onehot_low = onehot_full.astype(jnp.bfloat16)
    live = valid.astype(jnp.bfloat16)
    count_terms = jnp.dot(live[None, :], onehot_low, preferred_element_type=jnp.float32)[0]
    whole = lax.all_gather(slopes, "layer", axis=0, tiled=True)
    masked = whole * live[None, :]
    sums = jnp.dot(masked, onehot_low, preferred_element_type=jnp.float32)
    sums, counts = (
        taken_together(sums.astype(jnp.bfloat16), "sens").astype(jnp.float32),
        taken_together(count_terms.astype(jnp.bfloat16), "sens").astype(jnp.float32),
    )
    clean = cleaned(whole, live, onehot_full, sums, counts)
    partial_points = contract(clean, reconstructor)
    points = summed_on_arrival(partial_points.astype(jnp.bfloat16), "sens", 0).astype(jnp.bfloat16)
    partial_commands = contract(points, lax.all_gather(fitting, "sens", axis=0, tiled=True))
    return summed_on_arrival(partial_commands.astype(jnp.bfloat16), "layer", 0)


def solution(mesh):
    placed = (P("layer", "sens"), P("sens"), P("sens"), P("layer", "sens"), P("sens", "layer"))
    return jax.shard_map(
        per_device,
        mesh=mesh,
        in_specs=placed,
        out_specs=P(("sens", "layer"), None),
        check_vma=False,
    )
```

profile of v0, /device:TPU:0, one launch (start us, length us, event | category | flops | bytes accessed | tf_op | source)
XLA Modules:
  0.0 284.0 jit_solution(14590893099064575598)
XLA Ops:
  6.5 0.7 all-gather.4.cloned.1.call-update
  7.3 0.0 all-gather.6.cloned.1.call-start
  7.3 0.7 all-gather.6.cloned.1.call-update
  8.0 0.8 fusion.17
  8.8 0.2 fusion.6
  9.0 10.5 %all_to_all.21 = bf16[8,1,12]{2,1,0:T(2,128)(2,1)S(1)} all-to-all(bf16[8,1,12]{2,1,0:T(2,128)(2,1)S(1)} %broadcast_in_dim.5), channel_id=1, replica_groups=mesh['sens'=8,'layer'=16] {'sens'}, dimensions={0} | all-to-all | bytes 384 | tf_op jit(solution)/shard_map/all_to_all | solution.py:11
  19.5 102.3 %all-gather.4.cloned.1.call-done = bf16[1024,7950]{1,0:T(8,128)(2,1)} async-done(((bf16[64,7950]{1,0:T(8,128)(2,1)}), bf16[1024,7950]{1,0:T(8,128)(2,1)}) %all-gather.4.cloned.1.call-update) | async-done | bytes 16281616 | tf_op jit(solution)/shard_map/all_gather | solution.py:57
  121.9 10.0 %fusion.3 = bf16[1024,12]{0,1:T(8,128)(2,1)S(1)} fusion(bf16[1024,7950]{1,0:T(8,128)(2,1)} %all-gather.4.cloned.1.call-done, bf16[7950]{0:T(1024)(128)(2,1)S(1)} %get-tuple-element.6, s32[7950]{0:T(1024)S(1)} %get-tuple-element.7), kind=kOutput, calls=%fused_computation.8 | convolution fusion | flops 203818496 | bytes 16353876 | tf_op jit(solution)/shard_map/dot_general | solution.py:59
  131.9 0.8 broadcast_in_dim.4
  132.7 4.4 %all-to-all-start = ((bf16[8,1024,12]{1,2,0:T(8,128)(2,1)}), bf16[8,1024,12]{1,2,0:T(8,128)(2,1)S(1)}, u32[]{:S(2)}, u32[]{:S(2)}) async-start(bf16[8,1024,12]{1,2,0:T(8,128)(2,1)} %broadcast_in_dim.4), calls=%async_computation | async-start | bytes 524288 | tf_op jit(solution)/shard_map/all_to_all | solution.py:11
  137.1 22.4 %copy.24 = bf16[1024,7950]{0,1:T(8,128)(2,1)} copy(bf16[1024,7950]{1,0:T(8,128)(2,1)} %all-gather.4.cloned.1.call-done) | data formatting | bytes 32563200 | tf_op jit(solution)/shard_map/all_gather | solution.py:57
  159.5 0.0 all-to-all-done
  159.6 19.0 %multiply_convert_fusion = bf16[1024,7950]{0,1:T(8,128)(2,1)S(1)} fusion(bf16[1024,7950]{0,1:T(8,128)(2,1)} %copy.24, f32[7950]{0:T(1024)S(1)} %get-tuple-element.5, s32[7950]{0:T(1024)S(1)} %get-tuple-element.7, f32[1024,12]{0,1:T(8,128)S(1)} %convert_reduce_fusion.1, f32[12]{0:T(128)S(1)} %broadcast_maximum_fusion), kind=kOutput, calls=%fused_computation | convolution fusion | flops 1204946048 | bytes 32676000 | tf_op jit(solution)/shard_map/dot_general | solution.py:39
  178.5 20.7 %convert_bitcast_fusion = bf16[125,8,8,128]{3,2,1,0:T(8,128)(2,1)S(1)} fusion(bf16[1024,7950]{0,1:T(8,128)(2,1)S(1)} %multiply_convert_fusion, bf16[1000,7950]{1,0:T(8,128)(2,1)} %param.8), kind=kOutput, calls=%fused_computation.7 | convolution fusion | flops 16282624000 | bytes 34229600 | tf_op jit(solution)/shard_map/dot_general | solution.py:32
  199.3 1.6 copy.33
  200.9 4.7 %all-to-all-start.2 = ((bf16[8,128,1000]{1,2,0:T(8,128)(2,1)}), bf16[8,128,1000]{1,2,0:T(8,128)(2,1)S(1)}, u32[]{:S(2)}, u32[]{:S(2)}) async-start(bf16[8,128,1000]{1,2,0:T(8,128)(2,1)} %bitcast.16), calls=%async_computation.2 | async-start | bytes 4096000 | tf_op jit(solution)/shard_map/all_to_all | solution.py:27
  205.7 2.3 all-gather.6.cloned.1.call-done
  208.0 20.5 %reshape.30 = bf16[7800,1000]{1,0:T(8,128)(2,1)} reshape(bf16[8,975,1000]{2,1,0:T(8,128)(2,1)} %all-gather.6.cloned.1.call-done) | data formatting | bytes 31200000
  228.5 3.8 %all-to-all-done.2 = bf16[8,128,1000]{1,2,0:T(8,128)(2,1)S(1)} async-done(((bf16[8,128,1000]{1,2,0:T(8,128)(2,1)}), bf16[8,128,1000]{1,2,0:T(8,128)(2,1)S(1)}, u32[]{:S(2)}, u32[]{:S(2)}) %all-to-all-start.2) | async-done | bytes 2048032 | tf_op jit(solution)/shard_map/all_to_all | solution.py:27
  232.3 0.4 reduce_sum.41
  232.7 9.3 %convolution_convert_fusion = bf16[128,7800]{0,1:T(8,128)(2,1)} fusion(bf16[128,1000]{0,1:T(8,128)(2,1)S(1)} %reduce_sum.41, bf16[7800,1000]{1,0:T(8,128)(2,1)} %reshape.30), kind=kOutput, calls=%fused_computation.3 | convolution fusion | flops 1997798400 | bytes 17852800 | tf_op jit(solution)/shard_map/dot_general | solution.py:32
  242.0 2.9 %copy.28 = bf16[128,7800]{1,0:T(8,128)(2,1)S(1)} copy(bf16[128,7800]{0,1:T(8,128)(2,1)} %convolution_convert_fusion) | data formatting | bytes 3993600 | tf_op jit(solution)/shard_map/convert_element_type | solution.py:68
  244.9 31.2 %all_to_all.22 = bf16[16,8,7800]{2,1,0:T(8,128)(2,1)S(1)} all-to-all(bf16[16,8,7800]{2,1,0:T(8,128)(2,1)S(1)} %bitcast.17), channel_id=1, replica_groups=mesh['sens'=8,'layer'=16] {'layer'}, dimensions={0} | all-to-all | bytes 3993600 | tf_op jit(solution)/shard_map/all_to_all | solution.py:27
  276.2 1.0 convert_reduce_fusion
  (6 shorter events, 0.1 us)
Async XLA Ops:
  6.5 115.3 %all-gather.4.cloned.1.call-start = ((), (), s32[]{:S(2)}) async-start(), calls=%async_computation.4 | async-start | bytes 17547264 | tf_op jit(solution)/shard_map/all_gather | solution.py:57
  7.3 200.7 %all-gather.6.cloned.1.call-start = ((), (), s32[]{:S(2)}) async-start(), calls=%async_computation.5 | async-start | bytes 17989632 | tf_op jit(solution)/shard_map/all_gather | solution.py:67
  132.7 26.8 %all-to-all-start = ((bf16[8,1024,12]{1,2,0:T(8,128)(2,1)}), bf16[8,1024,12]{1,2,0:T(8,128)(2,1)S(1)}, u32[]{:S(2)}, u32[]{:S(2)}) async-start(bf16[8,1024,12]{1,2,0:T(8,128)(2,1)} %broadcast_in_dim.4), calls=%async_computation | async-start | bytes 524288 | tf_op jit(solution)/shard_map/all_to_all | solution.py:11
  200.9 31.4 %all-to-all-start.2 = ((bf16[8,128,1000]{1,2,0:T(8,128)(2,1)}), bf16[8,128,1000]{1,2,0:T(8,128)(2,1)S(1)}, u32[]{:S(2)}, u32[]{:S(2)}) async-start(bf16[8,128,1000]{1,2,0:T(8,128)(2,1)} %bitcast.16), calls=%async_computation.2 | async-start | bytes 4096000 | tf_op jit(solution)/shard_map/all_to_all | solution.py:27
Sparse Core Ops, SparseCore 0:
  9.5 112.3 all-gather.3
  123.5 84.3 all-gather.5
where the time goes:
time: 285 us; the launch traced here: 284 us
  waiting for transfers between devices  110 us (39%)
  matrix products  59.2 us (21%)
  local copies, waits for them, and re-layouts  48.3 us (17%)
  blocking collectives  41.7 us (15%)
  between operations  13.5 us (5%)
  starting transfers between devices  9.2 us (3%)
    all_gather x1, waiting for transfers between devices, per_device(): whole = lax.all_gather(slopes, 'layer', axis=0, tiled=True)  102 us
    all_to_all x1, blocking collectives, summed_on_arrival(): lax.all_to_all(blocks, axis, split_axis=0, concat_axis=0, tiled=True)  31.2 us
    dot_general x2, matrix products, contract(): lax.dot_general(left, right, (((1,), (1,)), ((), ())), preferred_element_...  30 us
    all_gather x1, local copies, waits for them, and re-layouts, per_device(): whole = lax.all_gather(slopes, 'layer', axis=0, tiled=True)  22.4 us
    unnamed x1, local copies, waits for them, and re-layouts  20.5 us
    dot_general x1, matrix products, cleaned(): lax.dot_general(means, onehot_full, (((1,), (1,)), ((), ())), precision=l...  19 us
    all_to_all x1, blocking collectives, copy_for_each(): lax.all_to_all(jnp.broadcast_to(x[None], (length, *x.shape)), axis, 0, 0,...  10.5 us
    dot_general x1, matrix products, per_device(): sums = jnp.dot(masked, onehot_low, preferred_element_type=jnp.float32)  10 us
  transfers between devices with their start and end apart: 4, of which 3 were waited for; matrix products, arithmetic and copies ran while one was open for 34% of the time, Pallas kernels for 0%

commit v1 on v0

--- a/solution.py
+++ b/solution.py
@@ -4,6 +4,27 @@
 from jax.sharding import PartitionSpec as P
 
 SENSORS = 6
+
+
+def gather_around(x, axis, dim):
+    peers, index, rows = (lax.axis_size(axis), lax.axis_index(axis), x.shape[dim])
+    right = [(i, (i + 1) % peers) for i in range(peers)]
+    left = [(i, (i - 1) % peers) for i in range(peers)]
+    filled = jnp.zeros((*x.shape[:dim], peers * rows, *x.shape[dim + 1 :]), x.dtype)
+    filled = lax.dynamic_update_slice_in_dim(filled, x, index * rows, axis=dim)
+    from_left = from_right = x
+    half = peers // 2
+    for step in range(1, half + 1):
+        from_left = lax.ppermute(from_left, axis, right)
+        filled = lax.dynamic_update_slice_in_dim(
+            filled, from_left, (index - step) % peers * rows, axis=dim
+        )
+        if step < peers - half:
+            from_right = lax.ppermute(from_right, axis, left)
+            filled = lax.dynamic_update_slice_in_dim(
+                filled, from_right, (index + step) % peers * rows, axis=dim
+            )
+    return filled
 
 
 def copy_for_each(x, axis):
@@ -54,7 +75,7 @@
     onehot_low = onehot_full.astype(jnp.bfloat16)
     live = valid.astype(jnp.bfloat16)
     count_terms = jnp.dot(live[None, :], onehot_low, preferred_element_type=jnp.float32)[0]
-    whole = lax.all_gather(slopes, "layer", axis=0, tiled=True)
+    whole = gather_around(slopes, "layer", 0)
     masked = whole * live[None, :]
     sums = jnp.dot(masked, onehot_low, preferred_element_type=jnp.float32)
     sums, counts = (

time: 285 us -> 751 us (2.64); the launches traced: 284 us -> 736 us
  local copies, waits for them, and re-layouts: 48.3 us -> 399 us
  waiting for transfers between devices: 110 us -> 149 us
  starting transfers between devices: 9.2 us -> 47.6 us
  blocking collectives: 41.7 us -> 63.2 us
    dynamic_update_slice x0 -> x16, local copies, waits for them, and re-layouts: none -> 331 us  [the longest x8 165 us: gather_around(): lax.dynamic_update_slice_in_dim(filled, from_left, (index - step) % peers...]
    ppermute x0 -> x15, waiting for transfers between devices: none -> 141 us  [the longest x8 141 us: gather_around(): from_left = lax.ppermute(from_left, axis, right)]
    all_gather x1 -> x0, waiting for transfers between devices: 102 us -> none  [per_device(): whole = lax.all_gather(slopes, 'layer', axis=0, tiled=True)]
    ppermute x0 -> x15, starting transfers between devices: none -> 37.5 us  [the longest x7 35.8 us: gather_around(): from_right = lax.ppermute(from_right, axis, left)]
    ppermute x0 -> x15, local copies, waits for them, and re-layouts: none -> 34.4 us  [the longest x8 17.9 us: gather_around(): from_left = lax.ppermute(from_left, axis, right)]
    all_to_all x1 -> x2, blocking collectives: 31.2 us -> 63.2 us  [summed_on_arrival(): lax.all_to_all(blocks, axis, split_axis=0, concat_axis=0, tiled=True)]
    all_gather x1 -> x0, local copies, waits for them, and re-layouts: 22.4 us -> none  [per_device(): whole = lax.all_gather(slopes, 'layer', axis=0, tiled=True)]
    all_to_all x1 -> x0, blocking collectives: 10.5 us -> none  [copy_for_each(): lax.all_to_all(jnp.broadcast_to(x[None], (length, *x.shape)), axis, 0, 0,...]
  transfers between devices with their start and end apart: 4 -> 18, of which waited for: 3 -> 8; matrix products, arithmetic and copies ran while one was open for 34% -> 58% of each run, Pallas kernels for 0% -> 0%
where the time goes in v1:
time: 751 us; the launch traced here: 736 us
  local copies, waits for them, and re-layouts  399 us (53%)
  waiting for transfers between devices  149 us (20%)
  blocking collectives  63.2 us (8%)
  matrix products  60.3 us (8%)
  starting transfers between devices  47.6 us (6%)
  between operations  14.3 us (2%)
    dynamic_update_slice x8, local copies, waits for them, and re-layouts, gather_around(): lax.dynamic_update_slice_in_dim(filled, from_left, (index - step) % peers...  165 us
    dynamic_update_slice x7, local copies, waits for them, and re-layouts, gather_around(): lax.dynamic_update_slice_in_dim(filled, from_right, (index + step) % peer...  147 us
    ppermute x8, waiting for transfers between devices, gather_around(): from_left = lax.ppermute(from_left, axis, right)  141 us
    all_to_all x2, blocking collectives, summed_on_arrival(): lax.all_to_all(blocks, axis, split_axis=0, concat_axis=0, tiled=True)  63.2 us
    ppermute x7, starting transfers between devices, gather_around(): from_right = lax.ppermute(from_right, axis, left)  35.8 us
    dot_general x2, matrix products, contract(): lax.dot_general(left, right, (((1,), (1,)), ((), ())), preferred_element_...  35.2 us
    unnamed x24, local copies, waits for them, and re-layouts  22.9 us
    dynamic_update_slice x1, local copies, waits for them, and re-layouts, gather_around(): filled = lax.dynamic_update_slice_in_dim(filled, x, index * rows, axis=dim)  19.4 us
  transfers between devices with their start and end apart: 18, of which 8 were waited for; matrix products, arithmetic and copies ran while one was open for 58% of the time, Pallas kernels for 0%

profile of v1, /device:TPU:0, one launch (start us, length us, event | category | flops | bytes accessed | tf_op | source)
XLA Modules:
  0.0 736.4 jit_solution(10150333326073654602)
XLA Ops:
  12.7 22.9 %collective-permute-done = bf16[64,7950]{1,0:T(8,128)(2,1)S(1)} collective-permute-done((bf16[64,7950]{1,0:T(8,128)(2,1)}, bf16[64,7950]{1,0:T(8,128)(2,1)S(1)}, u32[]{:S(2)}, u32[]{:S(2)}) %collective-permute-start) | collective-permute-done | bytes 1017632 | tf_op jit(solution)/shard_map/ppermute | solution.py:18
  41.0 21.9 %collective-permute-done.2 = bf16[64,7950]{1,0:T(8,128)(2,1)S(1)} collective-permute-done((bf16[64,7950]{1,0:T(8,128)(2,1)S(1)}, bf16[64,7950]{1,0:T(8,128)(2,1)S(1)}, u32[]{:S(2)}, u32[]{:S(2)}) %collective-permute-start.2) | collective-permute-done | bytes 1017632 | tf_op jit(solution)/shard_map/ppermute | solution.py:18
  68.3 21.0 %collective-permute-done.4 = bf16[64,7950]{1,0:T(8,128)(2,1)S(1)} collective-permute-done((bf16[64,7950]{1,0:T(8,128)(2,1)S(1)}, bf16[64,7950]{1,0:T(8,128)(2,1)S(1)}, u32[]{:S(2)}, u32[]{:S(2)}) %collective-permute-start.4) | collective-permute-done | bytes 1017632 | tf_op jit(solution)/shard_map/ppermute | solution.py:18
  94.6 20.1 %collective-permute-done.6 = bf16[64,7950]{1,0:T(8,128)(2,1)S(1)} collective-permute-done((bf16[64,7950]{1,0:T(8,128)(2,1)S(1)}, bf16[64,7950]{1,0:T(8,128)(2,1)S(1)}, u32[]{:S(2)}, u32[]{:S(2)}) %collective-permute-start.6) | collective-permute-done | bytes 1017632 | tf_op jit(solution)/shard_map/ppermute | solution.py:18
  120.0 19.1 %collective-permute-done.8 = bf16[64,7950]{1,0:T(8,128)(2,1)S(1)} collective-permute-done((bf16[64,7950]{1,0:T(8,128)(2,1)S(1)}, bf16[64,7950]{1,0:T(8,128)(2,1)S(1)}, u32[]{:S(2)}, u32[]{:S(2)}) %collective-permute-start.8) | collective-permute-done | bytes 1017632 | tf_op jit(solution)/shard_map/ppermute | solution.py:18
  202.0 19.4 %dynamic_update_slice.48 = bf16[1024,7950]{0,1:T(8,128)(2,1)} dynamic-update-slice(bf16[1024,7950]{0,1:T(8,128)(2,1)} %broadcast_in_dim.6, bf16[64,7950]{0,1:T(8,128)(2,1)S(1)} %copy.71, s32[]{:T(128)S(6)} %select_n.117, s32[]{:T(128)} %constant.111.clone.1) | dynamic-update-slice | bytes 2035204 | tf_op jit(solution)/shard_map/dynamic_update_slice | solution.py:14
  223.8 21.4 %dynamic_update_slice.49 = bf16[1024,7950]{0,1:T(8,128)(2,1)} dynamic-update-slice(bf16[1024,7950]{0,1:T(8,128)(2,1)} %dynamic_update_slice.48, bf16[64,7950]{0,1:T(8,128)(2,1)S(1)} %copy.72, s32[]{:T(128)S(6)} %select_n.119, s32[]{:T(128)} %constant.111.clone.1) | dynamic-update-slice | bytes 2035204 | tf_op jit(solution)/shard_map/dynamic_update_slice | solution.py:19
  247.6 22.3 %dynamic_update_slice.50 = bf16[1024,7950]{0,1:T(8,128)(2,1)} dynamic-update-slice(bf16[1024,7950]{0,1:T(8,128)(2,1)} %dynamic_update_slice.49, bf16[64,7950]{0,1:T(8,128)(2,1)S(1)} %copy.73, s32[]{:T(128)S(6)} %select_n.121, s32[]{:T(128)} %constant.111.clone.1) | dynamic-update-slice | bytes 2035204 | tf_op jit(solution)/shard_map/dynamic_update_slice | solution.py:24
  292.6 19.3 %dynamic_update_slice.52 = bf16[1024,7950]{0,1:T(8,128)(2,1)} dynamic-update-slice(bf16[1024,7950]{0,1:T(8,128)(2,1)} %dynamic_update_slice.51, bf16[64,7950]{0,1:T(8,128)(2,1)S(1)} %copy.75, s32[]{:T(128)S(6)} %select_n.125, s32[]{:T(128)} %constant.111.clone.1) | dynamic-update-slice | bytes 2035204 | tf_op jit(solution)/shard_map/dynamic_update_slice | solution.py:24
  314.3 22.2 %dynamic_update_slice.53 = bf16[1024,7950]{0,1:T(8,128)(2,1)} dynamic-update-slice(bf16[1024,7950]{0,1:T(8,128)(2,1)} %dynamic_update_slice.52, bf16[64,7950]{0,1:T(8,128)(2,1)S(1)} %copy.76, s32[]{:T(128)S(6)} %select_n.127, s32[]{:T(128)} %constant.111.clone.1) | dynamic-update-slice | bytes 2035204 | tf_op jit(solution)/shard_map/dynamic_update_slice | solution.py:19
  338.9 22.3 %dynamic_update_slice.54 = bf16[1024,7950]{0,1:T(8,128)(2,1)} dynamic-update-slice(bf16[1024,7950]{0,1:T(8,128)(2,1)} %dynamic_update_slice.53, bf16[64,7950]{0,1:T(8,128)(2,1)S(1)} %copy.77, s32[]{:T(128)S(6)} %select_n.129, s32[]{:T(128)} %constant.111.clone.1) | dynamic-update-slice | bytes 2035204 | tf_op jit(solution)/shard_map/dynamic_update_slice | solution.py:24
  363.5 19.4 %dynamic_update_slice.55 = bf16[1024,7950]{0,1:T(8,128)(2,1)} dynamic-update-slice(bf16[1024,7950]{0,1:T(8,128)(2,1)} %dynamic_update_slice.54, bf16[64,7950]{0,1:T(8,128)(2,1)S(1)} %copy.78, s32[]{:T(128)S(6)} %select_n.131, s32[]{:T(128)} %constant.111.clone.1) | dynamic-update-slice | bytes 2035204 | tf_op jit(solution)/shard_map/dynamic_update_slice | solution.py:19
  385.3 19.4 %dynamic_update_slice.56 = bf16[1024,7950]{0,1:T(8,128)(2,1)} dynamic-update-slice(bf16[1024,7950]{0,1:T(8,128)(2,1)} %dynamic_update_slice.55, bf16[64,7950]{0,1:T(8,128)(2,1)S(1)} %copy.79, s32[]{:T(128)S(6)} %select_n.133, s32[]{:T(128)} %constant.111.clone.1) | dynamic-update-slice | bytes 2035204 | tf_op jit(solution)/shard_map/dynamic_update_slice | solution.py:24
  407.0 22.3 %dynamic_update_slice.57 = bf16[1024,7950]{0,1:T(8,128)(2,1)} dynamic-update-slice(bf16[1024,7950]{0,1:T(8,128)(2,1)} %dynamic_update_slice.56, bf16[64,7950]{0,1:T(8,128)(2,1)S(1)} %copy.80, s32[]{:T(128)S(6)} %select_n.135, s32[]{:T(128)} %constant.111.clone.1) | dynamic-update-slice | bytes 2035204 | tf_op jit(solution)/shard_map/dynamic_update_slice | solution.py:19
  431.6 22.3 %dynamic_update_slice.58 = bf16[1024,7950]{0,1:T(8,128)(2,1)} dynamic-update-slice(bf16[1024,7950]{0,1:T(8,128)(2,1)} %dynamic_update_slice.57, bf16[64,7950]{0,1:T(8,128)(2,1)S(1)} %copy.81, s32[]{:T(128)S(6)} %select_n.137, s32[]{:T(128)} %constant.111.clone.1) | dynamic-update-slice | bytes 2035204 | tf_op jit(solution)/shard_map/dynamic_update_slice | solution.py:24
  456.2 19.4 %dynamic_update_slice.59 = bf16[1024,7950]{0,1:T(8,128)(2,1)} dynamic-update-slice(bf16[1024,7950]{0,1:T(8,128)(2,1)} %dynamic_update_slice.58, bf16[64,7950]{0,1:T(8,128)(2,1)S(1)} %copy.82, s32[]{:T(128)S(6)} %select_n.139, s32[]{:T(128)} %constant.111.clone.1) | dynamic-update-slice | bytes 2035204 | tf_op jit(solution)/shard_map/dynamic_update_slice | solution.py:19
  478.0 19.3 %dynamic_update_slice.60 = bf16[1024,7950]{0,1:T(8,128)(2,1)} dynamic-update-slice(bf16[1024,7950]{0,1:T(8,128)(2,1)} %dynamic_update_slice.59, bf16[64,7950]{0,1:T(8,128)(2,1)S(1)} %copy.83, s32[]{:T(128)S(6)} %select_n.141, s32[]{:T(128)} %constant.111.clone.1) | dynamic-update-slice | bytes 2035204 | tf_op jit(solution)/shard_map/dynamic_update_slice | solution.py:24
  498.8 22.4 %dynamic_update_slice.61 = bf16[1024,7950]{0,1:T(8,128)(2,1)} dynamic-update-slice(bf16[1024,7950]{0,1:T(8,128)(2,1)} %dynamic_update_slice.60, bf16[64,7950]{0,1:T(8,128)(2,1)S(1)} %copy.84, s32[]{:T(128)S(6)} %select_n.143, s32[]{:T(128)} %constant.111.clone.1) | dynamic-update-slice | bytes 2035204 | tf_op jit(solution)/shard_map/dynamic_update_slice | solution.py:19
  523.6 22.3 %dynamic_update_slice.62 = bf16[1024,7950]{0,1:T(8,128)(2,1)} dynamic-update-slice(bf16[1024,7950]{0,1:T(8,128)(2,1)} %dynamic_update_slice.61, bf16[64,7950]{0,1:T(8,128)(2,1)S(1)} %copy.85, s32[]{:T(128)S(6)} %select_n.145, s32[]{:T(128)} %constant.111.clone.1) | dynamic-update-slice | bytes 2035204 | tf_op jit(solution)/shard_map/dynamic_update_slice | solution.py:24
  548.3 19.4 %dynamic_update_slice.63 = bf16[1024,7950]{0,1:T(8,128)(2,1)} dynamic-update-slice(bf16[1024,7950]{0,1:T(8,128)(2,1)} %dynamic_update_slice.62, bf16[64,7950]{0,1:T(8,128)(2,1)S(1)} %copy.86, s32[]{:T(128)S(6)} %select_n.147, s32[]{:T(128)} %constant.111.clone.1) | dynamic-update-slice | bytes 2035204 | tf_op jit(solution)/shard_map/dynamic_update_slice | solution.py:19
  605.8 26.0 %convert_bitcast_fusion = bf16[125,8,8,128]{3,2,1,0:T(8,128)(2,1)S(1)} fusion(bf16[1000,7950]{1,0:T(8,128)(2,1)} %param.8, f32[1024,7950]{0,1:T(8,128)} %fusion.9, bf16[1024,7950]{0,1:T(8,128)(2,1)} %dynamic_update_slice.63, f32[7950]{0:T(1024)S(1)} %get-tuple-element.5), kind=kOutput, calls=%fused_computation.9 | convolution fusion | flops 16315187200 | bytes 66824600 | tf_op jit(solution)/shard_map/dot_general | solution.py:53
  632.1 29.6 %all_to_all.21 = bf16[8,128,1000]{1,2,0:T(8,128)(2,1)S(1)} all-to-all(bf16[8,128,1000]{1,2,0:T(8,128)(2,1)S(1)} %bitcast.15), channel_id=1, replica_groups=mesh['sens'=8,'layer'=16] {'sens'}, dimensions={0} | all-to-all | bytes 4096000 | tf_op jit(solution)/shard_map/all_to_all | solution.py:48
  662.1 20.5 %reshape.30 = bf16[7800,1000]{1,0:T(8,128)(2,1)} reshape(bf16[8,975,1000]{2,1,0:T(8,128)(2,1)} %all-gather.3.cloned.1.call-done) | data formatting | bytes 31200000
  694.8 33.5 %all_to_all.22 = bf16[16,8,7800]{2,1,0:T(8,128)(2,1)S(1)} all-to-all(bf16[16,8,7800]{2,1,0:T(8,128)(2,1)S(1)} %bitcast.16), channel_id=1, replica_groups=mesh['sens'=8,'layer'=16] {'layer'}, dimensions={0} | all-to-all | bytes 3993600 | tf_op jit(solution)/shard_map/all_to_all | solution.py:48
  (88 shorter events, 194.4 us)
Async XLA Ops:
  6.5 655.6 %all-gather.3.cloned.1.call-start = ((), (), s32[]{:S(2)}) async-start(), calls=%async_computation.4 | async-start | bytes 17989632 | tf_op jit(solution)/shard_map/all_gather | solution.py:88
  7.3 28.4 %collective-permute-start = (bf16[64,7950]{1,0:T(8,128)(2,1)}, bf16[64,7950]{1,0:T(8,128)(2,1)S(1)}, u32[]{:S(2)}, u32[]{:S(2)}) collective-permute-start(bf16[64,7950]{1,0:T(8,128)(2,1)} %param.5), channel_id=1, source_target_pairs={{0,1},{1,2},{2,3},{3,4},{4,5},{5,6},{6,7},{7,8},{8,9},{9,10},{10,1... | collective-permute-start | bytes 3052808 | tf_op jit(solution)/shard_map/ppermute | solution.py:18
  8.9 26.7 %collective-permute-start.1 = (bf16[64,7950]{1,0:T(8,128)(2,1)}, bf16[64,7950]{1,0:T(8,128)(2,1)S(1)}, u32[]{:S(2)}, u32[]{:S(2)}) collective-permute-start(bf16[64,7950]{1,0:T(8,128)(2,1)} %param.5), channel_id=1, source_target_pairs={{0,15},{1,0},{2,1},{3,2},{4,3},{5,4},{6,5},{7,6},{8,7},{9,8},{10,9... | collective-permute-start | bytes 3052808 | tf_op jit(solution)/shard_map/ppermute | solution.py:23
  35.6 150.1 %copy-start.2 = (bf16[64,7950]{1,0:T(8,128)(2,1)}, bf16[64,7950]{1,0:T(8,128)(2,1)S(1)}, u32[]{:S(2)}) copy-start(bf16[64,7950]{1,0:T(8,128)(2,1)S(1)} %collective-permute-done) | copy-start | bytes 3052804
  35.6 27.3 %collective-permute-start.2 = (bf16[64,7950]{1,0:T(8,128)(2,1)S(1)}, bf16[64,7950]{1,0:T(8,128)(2,1)S(1)}, u32[]{:S(2)}, u32[]{:S(2)}) collective-permute-start(bf16[64,7950]{1,0:T(8,128)(2,1)S(1)} %collective-permute-done), channel_id=1, source_target_pairs={{0,1},{1,2},{2,3},{3,4},{4,5},{5,6},{6,7},{7,8},{8,9},{9,10},{10,1... | collective-permute-start | bytes 3052808 | tf_op jit(solution)/shard_map/ppermute | solution.py:18
  35.6 150.1 %copy-start = (bf16[64,7950]{1,0:T(8,128)(2,1)}, bf16[64,7950]{1,0:T(8,128)(2,1)S(1)}, u32[]{:S(2)}) copy-start(bf16[64,7950]{1,0:T(8,128)(2,1)S(1)} %collective-permute-done.1) | copy-start | bytes 3052804
  35.7 27.2 %collective-permute-start.3 = (bf16[64,7950]{1,0:T(8,128)(2,1)S(1)}, bf16[64,7950]{1,0:T(8,128)(2,1)S(1)}, u32[]{:S(2)}, u32[]{:S(2)}) collective-permute-start(bf16[64,7950]{1,0:T(8,128)(2,1)S(1)} %collective-permute-done.1), channel_id=1, source_target_pairs={{0,15},{1,0},{2,1},{3,2},{4,3},{5,4},{6,5},{7,6},{8,7},{9,8},{10,9... | collective-permute-start | bytes 3052808 | tf_op jit(solution)/shard_map/ppermute | solution.py:23
  62.9 122.8 %copy-start.1 = (bf16[64,7950]{1,0:T(8,128)(2,1)}, bf16[64,7950]{1,0:T(8,128)(2,1)S(1)}, u32[]{:S(2)}) copy-start(bf16[64,7950]{1,0:T(8,128)(2,1)S(1)} %collective-permute-done.2) | copy-start | bytes 3052804
  62.9 26.3 %collective-permute-start.4 = (bf16[64,7950]{1,0:T(8,128)(2,1)S(1)}, bf16[64,7950]{1,0:T(8,128)(2,1)S(1)}, u32[]{:S(2)}, u32[]{:S(2)}) collective-permute-start(bf16[64,7950]{1,0:T(8,128)(2,1)S(1)} %collective-permute-done.2), channel_id=1, source_target_pairs={{0,1},{1,2},{2,3},{3,4},{4,5},{5,6},{6,7},{7,8},{8,9},{9,10},{10,1... | collective-permute-start | bytes 3052808 | tf_op jit(solution)/shard_map/ppermute | solution.py:18
  62.9 122.8 %copy-start.3 = (bf16[64,7950]{1,0:T(8,128)(2,1)}, bf16[64,7950]{1,0:T(8,128)(2,1)S(1)}, u32[]{:S(2)}) copy-start(bf16[64,7950]{1,0:T(8,128)(2,1)S(1)} %collective-permute-done.3) | copy-start | bytes 3052804
  62.9 26.3 %collective-permute-start.5 = (bf16[64,7950]{1,0:T(8,128)(2,1)S(1)}, bf16[64,7950]{1,0:T(8,128)(2,1)S(1)}, u32[]{:S(2)}, u32[]{:S(2)}) collective-permute-start(bf16[64,7950]{1,0:T(8,128)(2,1)S(1)} %collective-permute-done.3), channel_id=1, source_target_pairs={{0,15},{1,0},{2,1},{3,2},{4,3},{5,4},{6,5},{7,6},{8,7},{9,8},{10,9... | collective-permute-start | bytes 3052808 | tf_op jit(solution)/shard_map/ppermute | solution.py:23
  89.2 96.5 %copy-start.4 = (bf16[64,7950]{1,0:T(8,128)(2,1)}, bf16[64,7950]{1,0:T(8,128)(2,1)S(1)}, u32[]{:S(2)}) copy-start(bf16[64,7950]{1,0:T(8,128)(2,1)S(1)} %collective-permute-done.4) | copy-start | bytes 3052804
  89.2 25.4 %collective-permute-start.6 = (bf16[64,7950]{1,0:T(8,128)(2,1)S(1)}, bf16[64,7950]{1,0:T(8,128)(2,1)S(1)}, u32[]{:S(2)}, u32[]{:S(2)}) collective-permute-start(bf16[64,7950]{1,0:T(8,128)(2,1)S(1)} %collective-permute-done.4), channel_id=1, source_target_pairs={{0,1},{1,2},{2,3},{3,4},{4,5},{5,6},{6,7},{7,8},{8,9},{9,10},{10,1... | collective-permute-start | bytes 3052808 | tf_op jit(solution)/shard_map/ppermute | solution.py:18
  89.3 96.5 %copy-start.5 = (bf16[64,7950]{1,0:T(8,128)(2,1)}, bf16[64,7950]{1,0:T(8,128)(2,1)S(1)}, u32[]{:S(2)}) copy-start(bf16[64,7950]{1,0:T(8,128)(2,1)S(1)} %collective-permute-done.5) | copy-start | bytes 3052804
  89.3 25.4 %collective-permute-start.7 = (bf16[64,7950]{1,0:T(8,128)(2,1)S(1)}, bf16[64,7950]{1,0:T(8,128)(2,1)S(1)}, u32[]{:S(2)}, u32[]{:S(2)}) collective-permute-start(bf16[64,7950]{1,0:T(8,128)(2,1)S(1)} %collective-permute-done.5), channel_id=1, source_target_pairs={{0,15},{1,0},{2,1},{3,2},{4,3},{5,4},{6,5},{7,6},{8,7},{9,8},{10,9... | collective-permute-start | bytes 3052808 | tf_op jit(solution)/shard_map/ppermute | solution.py:23
  114.7 24.5 %collective-permute-start.8 = (bf16[64,7950]{1,0:T(8,128)(2,1)S(1)}, bf16[64,7950]{1,0:T(8,128)(2,1)S(1)}, u32[]{:S(2)}, u32[]{:S(2)}) collective-permute-start(bf16[64,7950]{1,0:T(8,128)(2,1)S(1)} %collective-permute-done.6), channel_id=1, source_target_pairs={{0,1},{1,2},{2,3},{3,4},{4,5},{5,6},{6,7},{7,8},{8,9},{9,10},{10,1... | collective-permute-start | bytes 3052808 | tf_op jit(solution)/shard_map/ppermute | solution.py:18
  114.7 24.5 %collective-permute-start.9 = (bf16[64,7950]{1,0:T(8,128)(2,1)S(1)}, bf16[64,7950]{1,0:T(8,128)(2,1)S(1)}, u32[]{:S(2)}, u32[]{:S(2)}) collective-permute-start(bf16[64,7950]{1,0:T(8,128)(2,1)S(1)} %collective-permute-done.7), channel_id=1, source_target_pairs={{0,15},{1,0},{2,1},{3,2},{4,3},{5,4},{6,5},{7,6},{8,7},{9,8},{10,9... | collective-permute-start | bytes 3052808 | tf_op jit(solution)/shard_map/ppermute | solution.py:23
  139.2 23.6 %collective-permute-start.10 = (bf16[64,7950]{1,0:T(8,128)(2,1)S(1)}, bf16[64,7950]{1,0:T(8,128)(2,1)S(1)}, u32[]{:S(2)}, u32[]{:S(2)}) collective-permute-start(bf16[64,7950]{1,0:T(8,128)(2,1)S(1)} %collective-permute-done.8), channel_id=1, source_target_pairs={{0,1},{1,2},{2,3},{3,4},{4,5},{5,6},{6,7},{7,8},{8,9},{9,10},{10,1... | collective-permute-start | bytes 3052808 | tf_op jit(solution)/shard_map/ppermute | solution.py:18
  139.2 23.6 %collective-permute-start.11 = (bf16[64,7950]{1,0:T(8,128)(2,1)S(1)}, bf16[64,7950]{1,0:T(8,128)(2,1)}, u32[]{:S(2)}, u32[]{:S(2)}) collective-permute-start(bf16[64,7950]{1,0:T(8,128)(2,1)S(1)} %collective-permute-done.9), channel_id=1, source_target_pairs={{0,15},{1,0},{2,1},{3,2},{4,3},{5,4},{6,5},{7,6},{8,7},{9,8},{10,9... | collective-permute-start | bytes 3052808 | tf_op jit(solution)/shard_map/ppermute | solution.py:23
  162.7 23.0 %collective-permute-start.12 = (bf16[64,7950]{1,0:T(8,128)(2,1)S(1)}, bf16[64,7950]{1,0:T(8,128)(2,1)S(1)}, u32[]{:S(2)}, u32[]{:S(2)}) collective-permute-start(bf16[64,7950]{1,0:T(8,128)(2,1)S(1)} %collective-permute-done.10), channel_id=1, source_target_pairs={{0,1},{1,2},{2,3},{3,4},{4,5},{5,6},{6,7},{7,8},{8,9},{9,10},{10,1... | collective-permute-start | bytes 3052808 | tf_op jit(solution)/shard_map/ppermute | solution.py:18
  162.7 358.5 %collective-permute-start.13 = (bf16[64,7950]{1,0:T(8,128)(2,1)}, bf16[64,7950]{1,0:T(8,128)(2,1)}, u32[]{:S(2)}, u32[]{:S(2)}) collective-permute-start(bf16[64,7950]{1,0:T(8,128)(2,1)} %collective-permute-done.11), channel_id=1, source_target_pairs={{0,15},{1,0},{2,1},{3,2},{4,3},{5,4},{6,5},{7,6},{8,7},{9,8},{10,9... | collective-permute-start | bytes 3052808 | tf_op jit(solution)/shard_map/ppermute | solution.py:23
  185.7 360.2 %collective-permute-start.14 = (bf16[64,7950]{1,0:T(8,128)(2,1)S(1)}, bf16[64,7950]{1,0:T(8,128)(2,1)}, u32[]{:S(2)}, u32[]{:S(2)}) collective-permute-start(bf16[64,7950]{1,0:T(8,128)(2,1)S(1)} %collective-permute-done.12), channel_id=1, source_target_pairs={{0,1},{1,2},{2,3},{3,4},{4,5},{5,6},{6,7},{7,8},{8,9},{9,10},{10,1... | collective-permute-start | bytes 3052808 | tf_op jit(solution)/shard_map/ppermute | solution.py:18
  188.2 33.2 %all-to-all-start.1 = ((bf16[8,1,12]{2,1,0:T(2,128)(2,1)}), bf16[8,1,12]{2,1,0:T(2,128)(2,1)S(1)}, u32[]{:S(2)}, u32[]{:S(2)}) async-start(bf16[8,1,12]{2,1,0:T(2,128)(2,1)} %broadcast_in_dim.8), calls=%async_computation.1 | async-start | bytes 8192 | tf_op jit(solution)/shard_map/all_to_all | solution.py:32
  576.5 12.3 %all-to-all-start = ((bf16[8,1024,12]{1,2,0:T(8,128)(2,1)}), bf16[8,1024,12]{1,2,0:T(8,128)(2,1)S(1)}, u32[]{:S(2)}, u32[]{:S(2)}) async-start(bf16[8,1024,12]{1,2,0:T(8,128)(2,1)} %broadcast_in_dim.7), calls=%async_computation | async-start | bytes 524288 | tf_op jit(solution)/shard_map/all_to_all | solution.py:32
  (5 other events, 258.5 us)
Sparse Core Ops, SparseCore 0:
  9.0 84.3 all-gather.2
